TPU v7x, 32 devices: a whole 2x2x4 slice. The times are simulated.
32 devices in a mesh: sub: 8 (over z, y), grp: 4 (over x, core).
Axes of the slice: x: 2, y: 2, z: 4, core: 2. Of those that a mesh axis runs over, the one named last changes fastest.
Arguments:
- stiffness: bfloat16 [8, 64, 5, 256, 256], P('sub', 'grp'), may hold values from -0.0012207031 to 0.0012207031
- deflation: bfloat16 [8, 64, 16384], P('sub', None, 'grp'), may hold values from -6 to 6
- off_map: int32 [8, 3], replicated, may hold values from -2 to 2, as said below
- need_map: int32 [8, 4, 3, 4], P(None, 'grp'), may hold values from 0 to 15, as said below
- place_map: int32 [8, 4, 3, 4], P('sub', 'grp'), may hold values from 0 to 15, as said below
Outputs:
- coarse: float32 [8, 256, 256], P('sub', 'grp')
Inputs may be any that keep to these rules, and one draw needn't show every extreme that they name: `off_map`: the 3 offsets of one row are distinct and nonzero. `need_map`: the 4 tile numbers of one row are distinct. `place_map`: the 4 tile numbers of one row are distinct.
All inputs are finite; a program needn't handle non-finite values.
Results may differ from a plain program's by a relative error of at most 0.0029.
Values may be sent and summed in bfloat16 or wider, within the bound.
A program may use at most 128 MiB of HBM per device.

v0:
```python
import functools

import jax
import jax.numpy as jnp
from jax import lax
from jax.experimental import pallas as pl
from jax.experimental.pallas import tpu as pltpu
from jax.sharding import PartitionSpec as P

RCH = 2
MESH = pl.DeviceIdType.MESH
OFFSETS = [value for value in range(-RCH, RCH + 1) if value != 0]
SEND_ORDER = sorted(OFFSETS, key=lambda value: (value < 0, abs(value)))
CHUNKS = 1
NT = (((1,), (1,)), ((), ()))


def dot_nt(lhs, rhs):
    return lax.dot_general(lhs, rhs, NT, preferred_element_type=jnp.float32)


def kernel(
    subs, layers, chunks, off_hbm, need_hbm, place_hbm, defl_ref, stiff_ref, out_ref,
    off_ref, need_ref, place_ref, a_buf, basis, image, own_tiles, outgoing, part, part_low, shares,
    in_sem, a_sem, sub_send, sub_recv, own_send, own_recv, rim_send, rim_recv, red_send, red_recv,
    *arrived,
):
    s = lax.axis_index("sub")
    g = lax.axis_index("grp")
    _, tiles, bands, rows, _ = stiff_ref.shape
    vectors = defl_ref.shape[1]
    slots = off_ref.shape[0]
    overlap = place_ref.shape[3]
    rim = bands // 2
    halo = rim * rows
    width = tiles * rows
    columns = vectors * (slots + 1)
    share = out_ref.shape[1]
    depth = vectors // chunks
    count = len(OFFSETS)
    has_left = g > 0
    has_right = g < layers - 1

    barrier = pltpu.get_barrier_semaphore()
    for offset in SEND_ORDER:
        pl.semaphore_signal(
            barrier, inc=1, device_id=(lax.rem(s + offset + subs, subs), g), device_id_type=MESH
        )
    for step in range(1, layers):
        pl.semaphore_signal(
            barrier, inc=1, device_id=(s, lax.rem(g + step, layers)), device_id_type=MESH
        )

    inputs = [
        pltpu.make_async_copy(off_hbm, off_ref, in_sem.at[0]),
        pltpu.make_async_copy(need_hbm, need_ref, in_sem.at[1]),
        pltpu.make_async_copy(place_hbm, place_ref, in_sem.at[2]),
        pltpu.make_async_copy(
            defl_ref.at[0], basis.at[0, :, pl.ds(halo, width)], in_sem.at[3]
        ),
    ]
    for copy in inputs:
        copy.start()

    def stiff_copy(t):
        return pltpu.make_async_copy(stiff_ref.at[0, t], a_buf.at[t], a_sem.at[t])

    edges = list(range(rim)) + list(range(tiles - rim, tiles))
    for t in list(range(rim, tiles - rim)) + edges:
        stiff_copy(t).start()

    for buffer in arrived:
        for k in range(count):
            buffer[k * (overlap + 1) + overlap] = jnp.zeros((depth, rows), buffer.dtype)

    @pl.when(jnp.logical_not(has_left))
    def _():
        basis[:, :, 0:halo] = jnp.zeros((slots + 1, vectors, halo), basis.dtype)

    @pl.when(jnp.logical_not(has_right))
    def _():
        basis[:, :, halo + width :] = jnp.zeros((slots + 1, vectors, halo), basis.dtype)

    for copy in inputs:
        copy.wait()
    for u in range(tiles):
        own_tiles[u] = basis[0, :, halo + u * rows : halo + (u + 1) * rows]
    for k, offset in enumerate(OFFSETS):
        target = lax.rem(s + offset + subs, subs)
        for o in range(overlap):
            tile = jnp.int32(0)
            for n in range(slots):
                match = (off_ref[n, target] == -offset).astype(jnp.int32)
                tile = tile + match * need_ref[0, n, o, target]
            outgoing[k, o] = own_tiles[tile]

    pl.semaphore_wait(barrier, count + layers - 1)

    def sub_copy(k, h):
        back = count - 1 - k
        return pltpu.make_async_remote_copy(
            src_ref=outgoing.at[k, :, pl.ds(h * depth, depth)],
            dst_ref=arrived[h].at[pl.ds(back * (overlap + 1), overlap)],
            send_sem=sub_send.at[h, k],
            recv_sem=sub_recv.at[h, back],
            device_id=(lax.rem(s + OFFSETS[k] + subs, subs), g),
            device_id_type=MESH,
        )

    for h in range(chunks):
        for offset in SEND_ORDER:
            sub_copy(OFFSETS.index(offset), h).start()

    def edge_copy(blocks, lines, to_left, send, recv):
        source, target = (halo, halo + width) if to_left else (width, 0)
        return pltpu.make_async_remote_copy(
            src_ref=basis.at[blocks, lines, pl.ds(source, halo)],
            dst_ref=basis.at[blocks, lines, pl.ds(target, halo)],
            send_sem=send.at[0 if to_left else 1],
            recv_sem=recv.at[1 if to_left else 0],
            device_id=(s, g - 1 if to_left else g + 1),
            device_id_type=MESH,
        )

    def own_copy(to_left):
        return edge_copy(pl.ds(0, 1), pl.ds(0, vectors), to_left, own_send, own_recv)

    def rim_copy(h):
        return lambda to_left: edge_copy(
            pl.ds(1, slots), pl.ds(h * depth, depth), to_left, rim_send.at[h], rim_recv.at[h]
        )

    def start_pair(make):
        @pl.when(has_left)
        def _():
            make(True).start()

        @pl.when(has_right)
        def _():
            make(False).start()

    def wait_pair(make):
        @pl.when(has_left)
        def _():
            make(False).wait_recv()
            make(True).wait_send()

        @pl.when(has_right)
        def _():
            make(True).wait_recv()
            make(False).wait_send()

    start_pair(own_copy)

    def column(t):
        return t * rows if isinstance(t, int) else pl.multiple_of(t * rows, rows)

    def image_of(t, blocks, lines):
        running = None
        for b in range(bands):
            window = basis[blocks, lines, pl.ds(column(t + b), rows)]
            shape = window.shape
            term = dot_nt(window.reshape(-1, rows), a_buf[t, b])
            running = term if running is None else running + term
        image[blocks, lines, pl.ds(column(t), rows)] = running.astype(image.dtype).reshape(shape)

    def own_step(t, carry):
        stiff_copy(t).wait()
        image_of(t, slice(0, 1), slice(0, vectors))
        return carry

    lax.fori_loop(rim, tiles - rim, own_step, 0, unroll=2)
    wait_pair(own_copy)
    for t in edges:
        stiff_copy(t).wait()
        image_of(t, slice(0, 1), slice(0, vectors))

    def place(h, u, n):
        offset = off_ref[n, s]
        position = offset + RCH - (offset > 0).astype(jnp.int32)
        found = position * (overlap + 1) + overlap
        for o in range(overlap):
            hit = (place_ref[0, n, 0, o] == u).astype(jnp.int32)
            found = found + (o - overlap) * hit
        lines = slice(h * depth, (h + 1) * depth)
        basis[n + 1, lines, pl.ds(halo + column(u), rows)] = arrived[h][found]

    for h in range(chunks):
        lines = slice(h * depth, (h + 1) * depth)
        for k in range(count):
            sub_copy(k, h).wait_recv()
        for u in edges:
            for n in range(slots):
                place(h, u, n)

        def place_step(u, carry):
            for n in range(slots):
                place(h, u, n)
            return carry

        lax.fori_loop(rim, tiles - rim, place_step, 0)
        start_pair(rim_copy(h))

        def rest_step(t, carry):
            image_of(t, slice(1, slots + 1), lines)
            return carry

        lax.fori_loop(rim, tiles - rim, rest_step, 0, unroll=tiles - 2 * rim)
    for h in range(chunks):
        for k in range(count):
            sub_copy(k, h).wait_send()

    def partial(first, last):
        left = basis[:, :, halo + first * rows : halo + last * rows]
        right = image[:, :, first * rows : last * rows]
        return dot_nt(left.reshape(columns, -1), right.reshape(columns, -1))

    for h in range(chunks):
        if h == chunks - 1:
            part[...] = partial(rim, tiles - rim)
        wait_pair(rim_copy(h))
        for t in edges:
            image_of(t, slice(1, slots + 1), slice(h * depth, (h + 1) * depth))
    total = part[...] + partial(0, rim) + partial(tiles - rim, tiles)
    part_low[...] = total.astype(part_low.dtype)
    part[...] = total

    red_copies = []
    for step in range(1, layers):
        peer = lax.rem(g + step, layers)
        red_copies.append(
            pltpu.make_async_remote_copy(
                src_ref=part_low.at[pl.ds(pl.multiple_of(peer * share, share), share)],
                dst_ref=shares.at[step - 1],
                send_sem=red_send.at[step - 1],
                recv_sem=red_recv.at[step - 1],
                device_id=(s, peer),
                device_id_type=MESH,
            )
        )
    for copy in red_copies:
        copy.start()
    for copy in red_copies:
        copy.wait()
    result = part[pl.ds(pl.multiple_of(g * share, share), share), :]
    for step in range(1, layers):
        result = result + shares[step - 1].astype(jnp.float32)
    out_ref[0] = result


def on_device(subs, layers, stiffness, deflation, off_map, need_map, place_map):
    _, tiles, bands, rows, _ = stiffness.shape
    _, vectors, width = deflation.shape
    slots, overlap = place_map.shape[2:]
    columns = vectors * (slots + 1)
    halo = (bands // 2) * rows
    share = columns // layers
    count = len(OFFSETS)
    chunks = CHUNKS
    low = deflation.dtype
    dma = pltpu.SemaphoreType.DMA
    tables = (
        off_map.T,
        need_map.transpose(1, 2, 3, 0),
        place_map.transpose(0, 2, 1, 3),
    )
    return pl.pallas_call(
        functools.partial(kernel, subs, layers, chunks),
        out_shape=pltpu.VMEM((1, share, columns), jnp.float32),
        in_specs=[pl.BlockSpec(memory_space=pl.ANY)] * 5,
        out_specs=pl.BlockSpec(memory_space=pltpu.VMEM),
        scratch_shapes=[
            *[pltpu.SMEM(table.shape, table.dtype) for table in tables],
            pltpu.VMEM((tiles, bands, rows, rows), low),
            pltpu.VMEM((slots + 1, vectors, width + 2 * halo), low),
            pltpu.VMEM((slots + 1, vectors, width), low),
            pltpu.VMEM((tiles, vectors, rows), low),
            pltpu.VMEM((count, overlap, vectors, rows), low),
            pltpu.VMEM((columns, columns), jnp.float32),
            pltpu.VMEM((columns, columns), low),
            pltpu.VMEM((layers - 1, share, columns), low),
            dma((4,)),
            dma((tiles,)),
            dma((chunks, count)), dma((chunks, count)),
            dma((2,)), dma((2,)),
            dma((chunks, 2)), dma((chunks, 2)),
            dma((layers - 1,)), dma((layers - 1,)),
            *[pltpu.VMEM((count * (overlap + 1), vectors // chunks, rows), low)] * chunks,
        ],
        compiler_params=pltpu.CompilerParams(collective_id=0, has_side_effects=True),
    )(*tables, deflation, stiffness)


def solution(mesh):
    in_specs = (
        P("sub", "grp", None, None, None),
        P("sub", None, "grp"),
        P(),
        P(None, "grp", None, None),
        P("sub", "grp", None, None),
    )
    out_specs = P("sub", "grp", None)
    return jax.shard_map(
        functools.partial(on_device, mesh.shape["sub"], mesh.shape["grp"]),
        mesh=mesh,
        in_specs=in_specs,
        out_specs=out_specs,
        check_vma=False,
    )
```

profile of v0, /device:TPU:0, one launch (start us, length us, event | category | flops | bytes accessed | tf_op | source)
XLA Modules:
  0.0 26.3 jit_solution(15001245659846039087)
XLA Ops:
  0.0 25.7 %shard_map.55 = f32[1,64,256]{2,1,0:T(8,128)S(1)} custom-call(s32[3,8]{1,0:T(4,128)} %bitcast.4, s32[1,3,4,8]{3,2,1,0:T(4,128)} %bitcast.3, s32[1,3,1,4]{3,2,1,0:T(1,128)} %bitcast.5, bf16[1,64,4096]{2,1,0:T(8,128)(2,1)} %defl_ref.1, bf16[1,16,5,256,256]{4,3,2,1,0:T(8,128)(2,1)} %stiff_ref.1), custom_call_target="tpu_custom_call" | custom-call | tf_op jit(solution)/shard_map/pallas_call | solution.py:267
  25.7 0.6 %copy.7 = f32[1,64,256]{2,1,0:T(8,128)} copy(f32[1,64,256]{2,1,0:T(8,128)S(1)} %shard_map.55) | data formatting | bytes 131072
where the time goes:
time: 26.4 us; the launch traced here: 26.3 us
  Pallas kernels  25.7 us (97%)
  local copies, waits for them, and re-layouts  0.63 us (2%)
    pallas_call x1, Pallas kernels, on_device(): pl.pallas_call(functools.partial(kernel, subs, layers, chunks), out_shape...  25.7 us
    unnamed x1, local copies, waits for them, and re-layouts  0.63 us

commit v1 on v0

--- a/solution.py
+++ b/solution.py
@@ -13,15 +13,20 @@
 SEND_ORDER = sorted(OFFSETS, key=lambda value: (value < 0, abs(value)))
 CHUNKS = 1
 NT = (((1,), (1,)), ((), ()))
+NN = (((1,), (0,)), ((), ()))
 
 
 def dot_nt(lhs, rhs):
     return lax.dot_general(lhs, rhs, NT, preferred_element_type=jnp.float32)
 
 
+def dot_nn(lhs, rhs):
+    return lax.dot_general(lhs, rhs, NN, preferred_element_type=jnp.float32)
+
+
 def kernel(
     subs, layers, chunks, off_hbm, need_hbm, place_hbm, defl_ref, stiff_ref, out_ref,
-    off_ref, need_ref, place_ref, a_buf, basis, image, own_tiles, outgoing, part, part_low, shares,
+    off_ref, need_ref, place_ref, a_buf, basis, image, left_image, own_tiles, outgoing, part, part_low, shares,
     in_sem, a_sem, sub_send, sub_recv, own_send, own_recv, rim_send, rim_recv, red_send, red_recv,
     *arrived,
 ):
@@ -66,8 +71,6 @@
         return pltpu.make_async_copy(stiff_ref.at[0, t], a_buf.at[t], a_sem.at[t])
 
     edges = list(range(rim)) + list(range(tiles - rim, tiles))
-    for t in list(range(rim, tiles - rim)) + edges:
-        stiff_copy(t).start()
 
     for buffer in arrived:
         for k in range(count):
@@ -83,6 +86,8 @@
 
     for copy in inputs:
         copy.wait()
+    for t in range(tiles):
+        stiff_copy(t).start()
     for u in range(tiles):
         own_tiles[u] = basis[0, :, halo + u * rows : halo + (u + 1) * rows]
     for k, offset in enumerate(OFFSETS):
@@ -155,25 +160,46 @@
     def column(t):
         return t * rows if isinstance(t, int) else pl.multiple_of(t * rows, rows)
 
-    def image_of(t, blocks, lines):
+    def image_of(t):
         running = None
         for b in range(bands):
-            window = basis[blocks, lines, pl.ds(column(t + b), rows)]
+            term = dot_nt(basis[0, :, pl.ds(column(t + b), rows)], a_buf[t, b])
+            running = term if running is None else running + term
+        image[:, pl.ds(column(t), rows)] = running.astype(image.dtype)
+
+    def left_of(c, blocks):
+        running = None
+        for b in range(bands):
+            t = c - b
+            if isinstance(t, int) and not 0 <= t < tiles:
+                continue
+            window = basis[blocks, :, pl.ds(column(t + rim), rows)]
             shape = window.shape
-            term = dot_nt(window.reshape(-1, rows), a_buf[t, b])
+            term = dot_nn(window.reshape(-1, rows), a_buf[t, b])
             running = term if running is None else running + term
-        image[blocks, lines, pl.ds(column(t), rows)] = running.astype(image.dtype).reshape(shape)
+        left_image[blocks, :, pl.ds(column(c), rows)] = running.astype(left_image.dtype).reshape(shape)
+
+    own_blocks, other_blocks = slice(0, 1), slice(1, slots + 1)
 
     def own_step(t, carry):
         stiff_copy(t).wait()
-        image_of(t, slice(0, 1), slice(0, vectors))
+        if not isinstance(t, int) or rim <= t < tiles - rim:
+            image_of(t)
+        left_of(t, own_blocks)
         return carry
 
-    lax.fori_loop(rim, tiles - rim, own_step, 0, unroll=2)
+    inside = range(bands - 1, tiles - rim)
+    for t in range(inside.start):
+        own_step(t, 0)
+    lax.fori_loop(inside.start, inside.stop, own_step, 0, unroll=2)
+    for t in range(inside.stop, tiles):
+        own_step(t, 0)
+    for c in range(tiles, tiles + 2 * rim):
+        left_of(c, own_blocks)
     wait_pair(own_copy)
     for t in edges:
-        stiff_copy(t).wait()
-        image_of(t, slice(0, 1), slice(0, vectors))
+        image_of(t)
+    part[0:vectors, 0:vectors] = dot_nt(basis[0, :, halo : halo + width], image[...])
 
     def place(h, u, n):
         offset = off_ref[n, s]
@@ -201,29 +227,33 @@
         lax.fori_loop(rim, tiles - rim, place_step, 0)
         start_pair(rim_copy(h))
 
-        def rest_step(t, carry):
-            image_of(t, slice(1, slots + 1), lines)
-            return carry
-
-        lax.fori_loop(rim, tiles - rim, rest_step, 0, unroll=tiles - 2 * rim)
+    for c in range(bands - 1):
+        left_of(c, other_blocks)
+
+    def rest_step(c, carry):
+        left_of(c, other_blocks)
+        return carry
+
+    lax.fori_loop(bands - 1, tiles, rest_step, 0, unroll=tiles - bands + 1)
+    for c in range(tiles, tiles + 2 * rim):
+        left_of(c, other_blocks)
     for h in range(chunks):
         for k in range(count):
             sub_copy(k, h).wait_send()
 
+    others = vectors * slots
+    below = basis[1:, :, halo : halo + width].reshape(others, width)
+    part[vectors:, 0:vectors] = dot_nt(below, image[...])
+
     def partial(first, last):
-        left = basis[:, :, halo + first * rows : halo + last * rows]
-        right = image[:, :, first * rows : last * rows]
-        return dot_nt(left.reshape(columns, -1), right.reshape(columns, -1))
-
+        lhs = left_image[:, :, first:last].reshape(columns, -1)
+        return dot_nt(lhs, basis[1:, :, first:last].reshape(others, -1))
+
+    part[:, vectors:] = partial(halo, halo + width)
     for h in range(chunks):
-        if h == chunks - 1:
-            part[...] = partial(rim, tiles - rim)
         wait_pair(rim_copy(h))
-        for t in edges:
-            image_of(t, slice(1, slots + 1), slice(h * depth, (h + 1) * depth))
-    total = part[...] + partial(0, rim) + partial(tiles - rim, tiles)
-    part_low[...] = total.astype(part_low.dtype)
-    part[...] = total
+    part[:, vectors:] += partial(0, halo) + partial(halo + width, width + 2 * halo)
+    part_low[...] = part[...].astype(part_low.dtype)
 
     red_copies = []
     for step in range(1, layers):
@@ -273,7 +303,8 @@
             *[pltpu.SMEM(table.shape, table.dtype) for table in tables],
             pltpu.VMEM((tiles, bands, rows, rows), low),
             pltpu.VMEM((slots + 1, vectors, width + 2 * halo), low),
-            pltpu.VMEM((slots + 1, vectors, width), low),
+            pltpu.VMEM((vectors, width), low),
+            pltpu.VMEM((slots + 1, vectors, width + 2 * halo), low),
             pltpu.VMEM((tiles, vectors, rows), low),
             pltpu.VMEM((count, overlap, vectors, rows), low),
             pltpu.VMEM((columns, columns), jnp.float32),

time: 26.4 us -> 23.8 us (0.902)
  Pallas kernels: 25.7 us -> 23 us
    pallas_call x1, Pallas kernels: 25.7 us -> 23 us  [on_device(): pl.pallas_call(functools.partial(kernel, subs, layers, chunks), out_shape...]
where the time goes in v1:
time: 23.8 us; the launch traced here: 23.6 us
  Pallas kernels  23 us (97%)
  local copies, waits for them, and re-layouts  0.63 us (3%)
    pallas_call x1, Pallas kernels, on_device(): pl.pallas_call(functools.partial(kernel, subs, layers, chunks), out_shape...  23 us
    unnamed x1, local copies, waits for them, and re-layouts  0.63 us

profile of v1, /device:TPU:0, one launch (start us, length us, event | category | flops | bytes accessed | tf_op | source)
XLA Modules:
  0.0 23.6 jit_solution(6754294370337297428)
XLA Ops:
  0.0 23.0 %shard_map.55 = f32[1,64,256]{2,1,0:T(8,128)S(1)} custom-call(s32[3,8]{1,0:T(4,128)} %bitcast.4, s32[1,3,4,8]{3,2,1,0:T(4,128)} %bitcast.3, s32[1,3,1,4]{3,2,1,0:T(1,128)} %bitcast.5, bf16[1,64,4096]{2,1,0:T(8,128)(2,1)} %defl_ref.1, bf16[1,16,5,256,256]{4,3,2,1,0:T(8,128)(2,1)} %stiff_ref.1), custom_call_target="tpu_custom_call" | custom-call | tf_op jit(solution)/shard_map/pallas_call | solution.py:297
  23.0 0.6 %copy.7 = f32[1,64,256]{2,1,0:T(8,128)} copy(f32[1,64,256]{2,1,0:T(8,128)S(1)} %shard_map.55) | data formatting | bytes 131072

commit v2 on v1

--- a/solution.py
+++ b/solution.py
@@ -165,46 +165,52 @@
         for b in range(bands):
             term = dot_nt(basis[0, :, pl.ds(column(t + b), rows)], a_buf[t, b])
             running = term if running is None else running + term
-        image[:, pl.ds(column(t), rows)] = running.astype(image.dtype)
-
-    def left_of(c, blocks):
+        image[t] = running.astype(image.dtype)
+
+    def left_of(c, blocks, lines):
         running = None
         for b in range(bands):
             t = c - b
             if isinstance(t, int) and not 0 <= t < tiles:
                 continue
             window = basis[blocks, :, pl.ds(column(t + rim), rows)]
-            shape = window.shape
             term = dot_nn(window.reshape(-1, rows), a_buf[t, b])
             running = term if running is None else running + term
-        left_image[blocks, :, pl.ds(column(c), rows)] = running.astype(left_image.dtype).reshape(shape)
-
-    own_blocks, other_blocks = slice(0, 1), slice(1, slots + 1)
+        left_image[c, lines] = running.astype(left_image.dtype)
+
+    own = slice(0, 1), slice(0, vectors)
+    others = slice(1, slots + 1), slice(vectors, columns)
 
     def own_step(t, carry):
         stiff_copy(t).wait()
         if not isinstance(t, int) or rim <= t < tiles - rim:
             image_of(t)
-        left_of(t, own_blocks)
+        left_of(t, *own)
         return carry
 
     inside = range(bands - 1, tiles - rim)
     for t in range(inside.start):
         own_step(t, 0)
-    lax.fori_loop(inside.start, inside.stop, own_step, 0, unroll=2)
+    lax.fori_loop(inside.start, inside.stop, own_step, 0, unroll=len(inside))
     for t in range(inside.stop, tiles):
         own_step(t, 0)
     for c in range(tiles, tiles + 2 * rim):
-        left_of(c, own_blocks)
+        left_of(c, *own)
     wait_pair(own_copy)
     for t in edges:
         image_of(t)
-    part[0:vectors, 0:vectors] = dot_nt(basis[0, :, halo : halo + width], image[...])
+    corner = None
+    for t in range(tiles):
+        term = dot_nt(basis[0, :, halo + t * rows : halo + (t + 1) * rows], image[t])
+        corner = term if corner is None else corner + term
+    part[0:vectors, 0:vectors] = corner
+
+    def first_of(n):
+        offset = off_ref[n, s]
+        return (offset + RCH - (offset > 0).astype(jnp.int32)) * (overlap + 1)
 
     def place(h, u, n):
-        offset = off_ref[n, s]
-        position = offset + RCH - (offset > 0).astype(jnp.int32)
-        found = position * (overlap + 1) + overlap
+        found = first_of(n) + overlap
         for o in range(overlap):
             hit = (place_ref[0, n, 0, o] == u).astype(jnp.int32)
             found = found + (o - overlap) * hit
@@ -228,31 +234,43 @@
         start_pair(rim_copy(h))
 
     for c in range(bands - 1):
-        left_of(c, other_blocks)
+        left_of(c, *others)
 
     def rest_step(c, carry):
-        left_of(c, other_blocks)
+        left_of(c, *others)
         return carry
 
     lax.fori_loop(bands - 1, tiles, rest_step, 0, unroll=tiles - bands + 1)
     for c in range(tiles, tiles + 2 * rim):
-        left_of(c, other_blocks)
+        left_of(c, *others)
     for h in range(chunks):
         for k in range(count):
             sub_copy(k, h).wait_send()
 
-    others = vectors * slots
-    below = basis[1:, :, halo : halo + width].reshape(others, width)
-    part[vectors:, 0:vectors] = dot_nt(below, image[...])
-
-    def partial(first, last):
-        lhs = left_image[:, :, first:last].reshape(columns, -1)
-        return dot_nt(lhs, basis[1:, :, first:last].reshape(others, -1))
-
-    part[:, vectors:] = partial(halo, halo + width)
+    for n in range(slots):
+        low = below = None
+        for o in range(overlap):
+            tile = jnp.concatenate([buffer[first_of(n) + o] for buffer in arrived])
+            spot = place_ref[0, n, 0, o]
+            term = dot_nt(tile, image[spot])
+            low = term if low is None else low + term
+            term = dot_nt(left_image[rim + spot], tile)
+            below = term if below is None else below + term
+        lines = slice((n + 1) * vectors, (n + 2) * vectors)
+        part[lines, 0:vectors] = low
+        part[:, lines] = below
+
+    def edge_partial(tile):
+        right = basis[1:, :, tile * rows : (tile + 1) * rows].reshape(-1, rows)
+        return dot_nt(left_image[tile], right)
+
     for h in range(chunks):
         wait_pair(rim_copy(h))
-    part[:, vectors:] += partial(0, halo) + partial(halo + width, width + 2 * halo)
+    sides = None
+    for tile in list(range(rim)) + list(range(tiles + rim, tiles + 2 * rim)):
+        term = edge_partial(tile)
+        sides = term if sides is None else sides + term
+    part[:, vectors:] += sides
     part_low[...] = part[...].astype(part_low.dtype)
 
     red_copies = []
@@ -303,8 +321,8 @@
             *[pltpu.SMEM(table.shape, table.dtype) for table in tables],
             pltpu.VMEM((tiles, bands, rows, rows), low),
             pltpu.VMEM((slots + 1, vectors, width + 2 * halo), low),
-            pltpu.VMEM((vectors, width), low),
-            pltpu.VMEM((slots + 1, vectors, width + 2 * halo), low),
+            pltpu.VMEM((tiles, vectors, rows), low),
+            pltpu.VMEM((tiles + 2 * (bands // 2), columns, rows), low),
             pltpu.VMEM((tiles, vectors, rows), low),
             pltpu.VMEM((count, overlap, vectors, rows), low),
             pltpu.VMEM((columns, columns), jnp.float32),

time: 23.8 us -> 23.3 us (0.979)
  Pallas kernels: 23 us -> 22.5 us
    pallas_call x1, Pallas kernels: 23 us -> 22.5 us  [on_device(): pl.pallas_call(functools.partial(kernel, subs, layers, chunks), out_shape...]
where the time goes in v2:
time: 23.3 us; the launch traced here: 23.2 us
  Pallas kernels  22.5 us (97%)
  local copies, waits for them, and re-layouts  0.63 us (3%)
    pallas_call x1, Pallas kernels, on_device(): pl.pallas_call(functools.partial(kernel, subs, layers, chunks), out_shape...  22.5 us
    unnamed x1, local copies, waits for them, and re-layouts  0.63 us

profile of v2, /device:TPU:0, one launch (start us, length us, event | category | flops | bytes accessed | tf_op | source)
XLA Modules:
  0.0 23.2 jit_solution(11281461703146408866)
XLA Ops:
  0.0 22.5 %shard_map.55 = f32[1,64,256]{2,1,0:T(8,128)S(1)} custom-call(s32[3,8]{1,0:T(4,128)} %bitcast.4, s32[1,3,4,8]{3,2,1,0:T(4,128)} %bitcast.3, s32[1,3,1,4]{3,2,1,0:T(1,128)} %bitcast.5, bf16[1,64,4096]{2,1,0:T(8,128)(2,1)} %defl_ref.1, bf16[1,16,5,256,256]{4,3,2,1,0:T(8,128)(2,1)} %stiff_ref.1), custom_call_target="tpu_custom_call" | custom-call | tf_op jit(solution)/shard_map/pallas_call | solution.py:315
  22.5 0.6 %copy.7 = f32[1,64,256]{2,1,0:T(8,128)} copy(f32[1,64,256]{2,1,0:T(8,128)S(1)} %shard_map.55) | data formatting | bytes 131072

commit v3 on v2

--- a/solution.py
+++ b/solution.py
@@ -11,7 +11,7 @@
 MESH = pl.DeviceIdType.MESH
 OFFSETS = [value for value in range(-RCH, RCH + 1) if value != 0]
 SEND_ORDER = sorted(OFFSETS, key=lambda value: (value < 0, abs(value)))
-CHUNKS = 1
+NEAR_FIRST = [1, 2, -2, -1]
 NT = (((1,), (1,)), ((), ()))
 NN = (((1,), (0,)), ((), ()))
 
@@ -25,10 +25,10 @@
 
 
 def kernel(
-    subs, layers, chunks, off_hbm, need_hbm, place_hbm, defl_ref, stiff_ref, out_ref,
-    off_ref, need_ref, place_ref, a_buf, basis, image, left_image, own_tiles, outgoing, part, part_low, shares,
+    subs, layers, off_hbm, need_hbm, place_hbm, defl_ref, stiff_ref, out_ref,
+    off_ref, need_ref, place_ref, a_buf, basis, image, left_image, own_tiles, outgoing, arrived,
+    rim_out, rim_in, found_at, rim_found_at, part, part_low, shares,
     in_sem, a_sem, sub_send, sub_recv, own_send, own_recv, rim_send, rim_recv, red_send, red_recv,
-    *arrived,
 ):
     s = lax.axis_index("sub")
     g = lax.axis_index("grp")
@@ -41,7 +41,6 @@
     width = tiles * rows
     columns = vectors * (slots + 1)
     share = out_ref.shape[1]
-    depth = vectors // chunks
     count = len(OFFSETS)
     has_left = g > 0
     has_right = g < layers - 1
@@ -72,17 +71,18 @@
 
     edges = list(range(rim)) + list(range(tiles - rim, tiles))
 
-    for buffer in arrived:
-        for k in range(count):
-            buffer[k * (overlap + 1) + overlap] = jnp.zeros((depth, rows), buffer.dtype)
+    for k in range(count):
+        arrived[k * (overlap + 1) + overlap] = jnp.zeros((vectors, rows), arrived.dtype)
 
     @pl.when(jnp.logical_not(has_left))
     def _():
-        basis[:, :, 0:halo] = jnp.zeros((slots + 1, vectors, halo), basis.dtype)
+        basis[0, :, 0:halo] = jnp.zeros((vectors, halo), basis.dtype)
+        rim_in[:, :, 0:halo] = jnp.zeros((count, vectors, halo), rim_in.dtype)
 
     @pl.when(jnp.logical_not(has_right))
     def _():
-        basis[:, :, halo + width :] = jnp.zeros((slots + 1, vectors, halo), basis.dtype)
+        basis[0, :, halo + width :] = jnp.zeros((vectors, halo), basis.dtype)
+        rim_in[:, :, halo:] = jnp.zeros((count, vectors, halo), rim_in.dtype)
 
     for copy in inputs:
         copy.wait()
@@ -101,39 +101,49 @@
 
     pl.semaphore_wait(barrier, count + layers - 1)
 
-    def sub_copy(k, h):
+    def sub_copy(k, offset):
         back = count - 1 - k
         return pltpu.make_async_remote_copy(
-            src_ref=outgoing.at[k, :, pl.ds(h * depth, depth)],
-            dst_ref=arrived[h].at[pl.ds(back * (overlap + 1), overlap)],
-            send_sem=sub_send.at[h, k],
-            recv_sem=sub_recv.at[h, back],
-            device_id=(lax.rem(s + OFFSETS[k] + subs, subs), g),
+            src_ref=outgoing.at[k],
+            dst_ref=arrived.at[pl.ds(back * (overlap + 1), overlap)],
+            send_sem=sub_send.at[k],
+            recv_sem=sub_recv.at[back],
+            device_id=(lax.rem(s + offset + subs, subs), g),
             device_id_type=MESH,
         )
 
-    for h in range(chunks):
-        for offset in SEND_ORDER:
-            sub_copy(OFFSETS.index(offset), h).start()
-
-    def edge_copy(blocks, lines, to_left, send, recv):
+    lower = s < subs // 2
+    for near, far in zip(NEAR_FIRST, SEND_ORDER):
+        k, offset = OFFSETS.index(near), near
+        if near != far:
+            k = jnp.where(lower, k, OFFSETS.index(far))
+            offset = jnp.where(lower, near, far)
+        sub_copy(k, offset).start()
+
+    def own_copy(to_left):
         source, target = (halo, halo + width) if to_left else (width, 0)
         return pltpu.make_async_remote_copy(
-            src_ref=basis.at[blocks, lines, pl.ds(source, halo)],
-            dst_ref=basis.at[blocks, lines, pl.ds(target, halo)],
-            send_sem=send.at[0 if to_left else 1],
-            recv_sem=recv.at[1 if to_left else 0],
+            src_ref=basis.at[0, :, pl.ds(source, halo)],
+            dst_ref=basis.at[0, :, pl.ds(target, halo)],
+            send_sem=own_send.at[0 if to_left else 1],
+            recv_sem=own_recv.at[1 if to_left else 0],
             device_id=(s, g - 1 if to_left else g + 1),
             device_id_type=MESH,
         )
 
-    def own_copy(to_left):
-        return edge_copy(pl.ds(0, 1), pl.ds(0, vectors), to_left, own_send, own_recv)
-
-    def rim_copy(h):
-        return lambda to_left: edge_copy(
-            pl.ds(1, slots), pl.ds(h * depth, depth), to_left, rim_send.at[h], rim_recv.at[h]
-        )
+    def rim_copy(k):
+        def make(to_left):
+            source, target = (0, halo) if to_left else (halo, 0)
+            return pltpu.make_async_remote_copy(
+                src_ref=rim_out.at[k, :, pl.ds(source, halo)],
+                dst_ref=rim_in.at[k, :, pl.ds(target, halo)],
+                send_sem=rim_send.at[k, 0 if to_left else 1],
+                recv_sem=rim_recv.at[k, 1 if to_left else 0],
+                device_id=(s, g - 1 if to_left else g + 1),
+                device_id_type=MESH,
+            )
+
+        return make
 
     def start_pair(make):
         @pl.when(has_left)
@@ -159,6 +169,10 @@
 
     def column(t):
         return t * rows if isinstance(t, int) else pl.multiple_of(t * rows, rows)
+
+    def first_of(n):
+        offset = off_ref[n, s]
+        return (offset + RCH - (offset > 0).astype(jnp.int32)) * (overlap + 1)
 
     def image_of(t):
         running = None
@@ -181,19 +195,33 @@
     own = slice(0, 1), slice(0, vectors)
     others = slice(1, slots + 1), slice(vectors, columns)
 
-    def own_step(t, carry):
-        stiff_copy(t).wait()
-        if not isinstance(t, int) or rim <= t < tiles - rim:
-            image_of(t)
-        left_of(t, *own)
-        return carry
-
-    inside = range(bands - 1, tiles - rim)
-    for t in range(inside.start):
-        own_step(t, 0)
-    lax.fori_loop(inside.start, inside.stop, own_step, 0, unroll=len(inside))
-    for t in range(inside.stop, tiles):
-        own_step(t, 0)
+    blank = overlap
+    hits = [
+        [[(place_ref[0, n, 0, o] == u).astype(jnp.int32) for o in range(overlap)] for n in range(slots)]
+        for u in range(tiles)
+    ]
+    shift = [
+        [sum((o - blank) * hits[u][n][o] for o in range(overlap)) for n in range(slots)]
+        for u in range(tiles)
+    ]
+    for n in range(slots):
+        for u in range(tiles):
+            found_at[n * tiles + u] = first_of(n) + blank + shift[u][n]
+    for k, offset in enumerate(OFFSETS):
+        for i, u in enumerate(edges):
+            spot = k * (overlap + 1) + blank
+            for n in range(slots):
+                spot = spot + (off_ref[n, s] == offset).astype(jnp.int32) * shift[u][n]
+            rim_found_at[k * len(edges) + i] = spot
+
+    group = bands - 1
+    for first in range(0, tiles, group):
+        for t in range(first, min(first + group, tiles)):
+            stiff_copy(t).wait()
+        for t in range(first, min(first + group, tiles)):
+            if rim <= t < tiles - rim:
+                image_of(t)
+            left_of(t, *own)
     for c in range(tiles, tiles + 2 * rim):
         left_of(c, *own)
     wait_pair(own_copy)
@@ -205,52 +233,30 @@
         corner = term if corner is None else corner + term
     part[0:vectors, 0:vectors] = corner
 
-    def first_of(n):
-        offset = off_ref[n, s]
-        return (offset + RCH - (offset > 0).astype(jnp.int32)) * (overlap + 1)
-
-    def place(h, u, n):
-        found = first_of(n) + overlap
-        for o in range(overlap):
-            hit = (place_ref[0, n, 0, o] == u).astype(jnp.int32)
-            found = found + (o - overlap) * hit
-        lines = slice(h * depth, (h + 1) * depth)
-        basis[n + 1, lines, pl.ds(halo + column(u), rows)] = arrived[h][found]
-
-    for h in range(chunks):
-        lines = slice(h * depth, (h + 1) * depth)
-        for k in range(count):
-            sub_copy(k, h).wait_recv()
-        for u in edges:
-            for n in range(slots):
-                place(h, u, n)
-
-        def place_step(u, carry):
-            for n in range(slots):
-                place(h, u, n)
-            return carry
-
-        lax.fori_loop(rim, tiles - rim, place_step, 0)
-        start_pair(rim_copy(h))
-
-    for c in range(bands - 1):
+    for k in reversed(range(count)):
+        sub_copy(count - 1 - k, OFFSETS[count - 1 - k]).wait_recv()
+        for i in range(len(edges)):
+            tile = jnp.zeros((vectors, rows), arrived.dtype)
+            for o in range(overlap):
+                spot = k * (overlap + 1) + o
+                tile = jnp.where(rim_found_at[k * len(edges) + i] == spot, arrived[spot], tile)
+            rim_out[k, :, i * rows : (i + 1) * rows] = tile
+        if k < count - 1:
+            start_pair(rim_copy(k + 1))
+    for u in range(tiles):
+        for n in range(slots):
+            spot = halo + u * rows
+            basis[n + 1, :, spot : spot + rows] = arrived[found_at[n * tiles + u]]
+    start_pair(rim_copy(0))
+    for c in range(tiles + 2 * rim):
         left_of(c, *others)
-
-    def rest_step(c, carry):
-        left_of(c, *others)
-        return carry
-
-    lax.fori_loop(bands - 1, tiles, rest_step, 0, unroll=tiles - bands + 1)
-    for c in range(tiles, tiles + 2 * rim):
-        left_of(c, *others)
-    for h in range(chunks):
-        for k in range(count):
-            sub_copy(k, h).wait_send()
+    for k in range(count):
+        sub_copy(k, OFFSETS[k]).wait_send()
 
     for n in range(slots):
         low = below = None
         for o in range(overlap):
-            tile = jnp.concatenate([buffer[first_of(n) + o] for buffer in arrived])
+            tile = arrived[first_of(n) + o]
             spot = place_ref[0, n, 0, o]
             term = dot_nt(tile, image[spot])
             low = term if low is None else low + term
@@ -260,15 +266,20 @@
         part[lines, 0:vectors] = low
         part[:, lines] = below
 
-    def edge_partial(tile):
-        right = basis[1:, :, tile * rows : (tile + 1) * rows].reshape(-1, rows)
-        return dot_nt(left_image[tile], right)
-
-    for h in range(chunks):
-        wait_pair(rim_copy(h))
+    def edge_partial(i):
+        right = jnp.concatenate(
+            [
+                rim_in[off_ref[n, s] + RCH - (off_ref[n, s] > 0).astype(jnp.int32), :, i * rows : (i + 1) * rows]
+                for n in range(slots)
+            ]
+        )
+        return dot_nt(left_image[i if i < rim else tiles + i], right)
+
+    for k in range(count):
+        wait_pair(rim_copy(k))
     sides = None
-    for tile in list(range(rim)) + list(range(tiles + rim, tiles + 2 * rim)):
-        term = edge_partial(tile)
+    for i in range(2 * rim):
+        term = edge_partial(i)
         sides = term if sides is None else sides + term
     part[:, vectors:] += sides
     part_low[...] = part[...].astype(part_low.dtype)
@@ -304,7 +315,6 @@
     halo = (bands // 2) * rows
     share = columns // layers
     count = len(OFFSETS)
-    chunks = CHUNKS
     low = deflation.dtype
     dma = pltpu.SemaphoreType.DMA
     tables = (
@@ -313,7 +323,7 @@
         place_map.transpose(0, 2, 1, 3),
     )
     return pl.pallas_call(
-        functools.partial(kernel, subs, layers, chunks),
+        functools.partial(kernel, subs, layers),
         out_shape=pltpu.VMEM((1, share, columns), jnp.float32),
         in_specs=[pl.BlockSpec(memory_space=pl.ANY)] * 5,
         out_specs=pl.BlockSpec(memory_space=pltpu.VMEM),
@@ -325,16 +335,20 @@
             pltpu.VMEM((tiles + 2 * (bands // 2), columns, rows), low),
             pltpu.VMEM((tiles, vectors, rows), low),
             pltpu.VMEM((count, overlap, vectors, rows), low),
+            pltpu.VMEM((count * (overlap + 1), vectors, rows), low),
+            pltpu.VMEM((count, vectors, 2 * halo), low),
+            pltpu.VMEM((count, vectors, 2 * halo), low),
+            pltpu.SMEM((slots * tiles,), jnp.int32),
+            pltpu.SMEM((count * 2 * (bands // 2),), jnp.int32),
             pltpu.VMEM((columns, columns), jnp.float32),
             pltpu.VMEM((columns, columns), low),
             pltpu.VMEM((layers - 1, share, columns), low),
             dma((4,)),
             dma((tiles,)),
-            dma((chunks, count)), dma((chunks, count)),
+            dma((count,)), dma((count,)),
             dma((2,)), dma((2,)),
-            dma((chunks, 2)), dma((chunks, 2)),
+            dma((count, 2)), dma((count, 2)),
             dma((layers - 1,)), dma((layers - 1,)),
-            *[pltpu.VMEM((count * (overlap + 1), vectors // chunks, rows), low)] * chunks,
         ],
         compiler_params=pltpu.CompilerParams(collective_id=0, has_side_effects=True),
     )(*tables, deflation, stiffness)

time: 23.3 us -> 23.7 us (1.017)
  the two profiles are of different devices: /device:TPU:0 before, /device:TPU:31 now
where the time goes in v3:
time: 23.7 us; the launch traced here: 23.5 us
  Pallas kernels  22.9 us (97%)
  local copies, waits for them, and re-layouts  0.63 us (3%)
    pallas_call x1, Pallas kernels, on_device(): pl.pallas_call(functools.partial(kernel, subs, layers), out_shape=pltpu.V...  22.9 us
    unnamed x1, local copies, waits for them, and re-layouts  0.63 us

profile of v3, /device:TPU:31, one launch (start us, length us, event | category | flops | bytes accessed | tf_op | source)
XLA Modules:
  0.0 23.5 jit_solution(9839139669638058315)
XLA Ops:
  0.0 22.9 %shard_map.55 = f32[1,64,256]{2,1,0:T(8,128)S(1)} custom-call(s32[3,8]{1,0:T(4,128)} %bitcast.4, s32[1,3,4,8]{3,2,1,0:T(4,128)} %bitcast.3, s32[1,3,1,4]{3,2,1,0:T(1,128)} %bitcast.5, bf16[1,64,4096]{2,1,0:T(8,128)(2,1)} %defl_ref.1, bf16[1,16,5,256,256]{4,3,2,1,0:T(8,128)(2,1)} %stiff_ref.1), custom_call_target="tpu_custom_call" | custom-call | tf_op jit(solution)/shard_map/pallas_call | solution.py:325
  22.9 0.6 %copy.7 = f32[1,64,256]{2,1,0:T(8,128)} copy(f32[1,64,256]{2,1,0:T(8,128)S(1)} %shard_map.55) | data formatting | bytes 131072

commit v4 on v3

--- a/solution.py
+++ b/solution.py
@@ -12,6 +12,7 @@
 OFFSETS = [value for value in range(-RCH, RCH + 1) if value != 0]
 SEND_ORDER = sorted(OFFSETS, key=lambda value: (value < 0, abs(value)))
 NEAR_FIRST = [1, 2, -2, -1]
+ARRIVALS = [OFFSETS.index(-value) for value in SEND_ORDER]
 NT = (((1,), (1,)), ((), ()))
 NN = (((1,), (0,)), ((), ()))
 
@@ -77,12 +78,12 @@
     @pl.when(jnp.logical_not(has_left))
     def _():
         basis[0, :, 0:halo] = jnp.zeros((vectors, halo), basis.dtype)
-        rim_in[:, :, 0:halo] = jnp.zeros((count, vectors, halo), rim_in.dtype)
+        rim_in[:, 0] = jnp.zeros((count, vectors, halo), rim_in.dtype)
 
     @pl.when(jnp.logical_not(has_right))
     def _():
         basis[0, :, halo + width :] = jnp.zeros((vectors, halo), basis.dtype)
-        rim_in[:, :, halo:] = jnp.zeros((count, vectors, halo), rim_in.dtype)
+        rim_in[:, 1] = jnp.zeros((count, vectors, halo), rim_in.dtype)
 
     for copy in inputs:
         copy.wait()
@@ -133,10 +134,10 @@
 
     def rim_copy(k):
         def make(to_left):
-            source, target = (0, halo) if to_left else (halo, 0)
+            source, target = (0, 1) if to_left else (1, 0)
             return pltpu.make_async_remote_copy(
-                src_ref=rim_out.at[k, :, pl.ds(source, halo)],
-                dst_ref=rim_in.at[k, :, pl.ds(target, halo)],
+                src_ref=rim_out.at[k, source],
+                dst_ref=rim_in.at[k, target],
                 send_sem=rim_send.at[k, 0 if to_left else 1],
                 recv_sem=rim_recv.at[k, 1 if to_left else 0],
                 device_id=(s, g - 1 if to_left else g + 1),
@@ -233,21 +234,22 @@
         corner = term if corner is None else corner + term
     part[0:vectors, 0:vectors] = corner
 
-    for k in reversed(range(count)):
+    for k in ARRIVALS:
         sub_copy(count - 1 - k, OFFSETS[count - 1 - k]).wait_recv()
         for i in range(len(edges)):
             tile = jnp.zeros((vectors, rows), arrived.dtype)
             for o in range(overlap):
                 spot = k * (overlap + 1) + o
                 tile = jnp.where(rim_found_at[k * len(edges) + i] == spot, arrived[spot], tile)
-            rim_out[k, :, i * rows : (i + 1) * rows] = tile
-        if k < count - 1:
-            start_pair(rim_copy(k + 1))
+            lane = i % rim * rows
+            rim_out[k, i // rim, :, lane : lane + rows] = tile
+        if k != ARRIVALS[0]:
+            start_pair(rim_copy(ARRIVALS[ARRIVALS.index(k) - 1]))
     for u in range(tiles):
         for n in range(slots):
             spot = halo + u * rows
             basis[n + 1, :, spot : spot + rows] = arrived[found_at[n * tiles + u]]
-    start_pair(rim_copy(0))
+    start_pair(rim_copy(ARRIVALS[-1]))
     for c in range(tiles + 2 * rim):
         left_of(c, *others)
     for k in range(count):
@@ -267,9 +269,10 @@
         part[:, lines] = below
 
     def edge_partial(i):
+        lane = i % rim * rows
         right = jnp.concatenate(
             [
-                rim_in[off_ref[n, s] + RCH - (off_ref[n, s] > 0).astype(jnp.int32), :, i * rows : (i + 1) * rows]
+                rim_in[off_ref[n, s] + RCH - (off_ref[n, s] > 0).astype(jnp.int32), i // rim, :, lane : lane + rows]
                 for n in range(slots)
             ]
         )
@@ -336,8 +339,8 @@
             pltpu.VMEM((tiles, vectors, rows), low),
             pltpu.VMEM((count, overlap, vectors, rows), low),
             pltpu.VMEM((count * (overlap + 1), vectors, rows), low),
-            pltpu.VMEM((count, vectors, 2 * halo), low),
-            pltpu.VMEM((count, vectors, 2 * halo), low),
+            pltpu.VMEM((count, 2, vectors, halo), low),
+            pltpu.VMEM((count, 2, vectors, halo), low),
             pltpu.SMEM((slots * tiles,), jnp.int32),
             pltpu.SMEM((count * 2 * (bands // 2),), jnp.int32),
             pltpu.VMEM((columns, columns), jnp.float32),

time: 23.7 us -> 22.6 us (0.954)
  the two profiles are of different devices: /device:TPU:31 before, /device:TPU:29 now
where the time goes in v4:
time: 22.6 us; the launch traced here: 22.5 us
  Pallas kernels  21.8 us (96%)
  local copies, waits for them, and re-layouts  0.63 us (3%)
    pallas_call x1, Pallas kernels, on_device(): pl.pallas_call(functools.partial(kernel, subs, layers), out_shape=pltpu.V...  21.8 us
    unnamed x1, local copies, waits for them, and re-layouts  0.63 us

profile of v4, /device:TPU:29, one launch (start us, length us, event | category | flops | bytes accessed | tf_op | source)
XLA Modules:
  0.0 22.5 jit_solution(2981568345449589956)
XLA Ops:
  0.0 21.8 %shard_map.55 = f32[1,64,256]{2,1,0:T(8,128)S(1)} custom-call(s32[3,8]{1,0:T(4,128)} %bitcast.4, s32[1,3,4,8]{3,2,1,0:T(4,128)} %bitcast.3, s32[1,3,1,4]{3,2,1,0:T(1,128)} %bitcast.5, bf16[1,64,4096]{2,1,0:T(8,128)(2,1)} %defl_ref.1, bf16[1,16,5,256,256]{4,3,2,1,0:T(8,128)(2,1)} %stiff_ref.1), custom_call_target="tpu_custom_call" | custom-call | tf_op jit(solution)/shard_map/pallas_call | solution.py:328
  21.8 0.6 %copy.7 = f32[1,64,256]{2,1,0:T(8,128)} copy(f32[1,64,256]{2,1,0:T(8,128)S(1)} %shard_map.55) | data formatting | bytes 131072

commit v5 on v4

--- a/solution.py
+++ b/solution.py
@@ -228,13 +228,7 @@
     wait_pair(own_copy)
     for t in edges:
         image_of(t)
-    corner = None
-    for t in range(tiles):
-        term = dot_nt(basis[0, :, halo + t * rows : halo + (t + 1) * rows], image[t])
-        corner = term if corner is None else corner + term
-    part[0:vectors, 0:vectors] = corner
-
-    for k in ARRIVALS:
+    def land(k):
         sub_copy(count - 1 - k, OFFSETS[count - 1 - k]).wait_recv()
         for i in range(len(edges)):
             tile = jnp.zeros((vectors, rows), arrived.dtype)
@@ -243,8 +237,26 @@
                 tile = jnp.where(rim_found_at[k * len(edges) + i] == spot, arrived[spot], tile)
             lane = i % rim * rows
             rim_out[k, i // rim, :, lane : lane + rows] = tile
-        if k != ARRIVALS[0]:
-            start_pair(rim_copy(ARRIVALS[ARRIVALS.index(k) - 1]))
+
+    def corner(first, last):
+        total = None
+        for t in range(first, last):
+            term = dot_nt(basis[0, :, halo + t * rows : halo + (t + 1) * rows], image[t])
+            total = term if total is None else total + term
+        return total
+
+    middle, early = tiles // 2, ARRIVALS[:2]
+    for k in early:
+        land(k)
+    part[0:vectors, 0:vectors] = corner(0, middle)
+    for k in early:
+        start_pair(rim_copy(k))
+    for k in ARRIVALS[2:-1]:
+        land(k)
+    part[0:vectors, 0:vectors] += corner(middle, tiles)
+    for k in ARRIVALS[2:-1]:
+        start_pair(rim_copy(k))
+    land(ARRIVALS[-1])
     for u in range(tiles):
         for n in range(slots):
             spot = halo + u * rows

time: 22.6 us -> 22.7 us (level)
  no operation moved by 1% of the time
where the time goes in v5:
time: 22.7 us; the launch traced here: 22.5 us
  Pallas kernels  21.9 us (96%)
  local copies, waits for them, and re-layouts  0.63 us (3%)
    pallas_call x1, Pallas kernels, on_device(): pl.pallas_call(functools.partial(kernel, subs, layers), out_shape=pltpu.V...  21.9 us
    unnamed x1, local copies, waits for them, and re-layouts  0.63 us

profile of v5, /device:TPU:29, one launch (start us, length us, event | category | flops | bytes accessed | tf_op | source)
XLA Modules:
  0.0 22.5 jit_solution(14868064353192577394)
XLA Ops:
  0.0 21.9 %shard_map.55 = f32[1,64,256]{2,1,0:T(8,128)S(1)} custom-call(s32[3,8]{1,0:T(4,128)} %bitcast.4, s32[1,3,4,8]{3,2,1,0:T(4,128)} %bitcast.3, s32[1,3,1,4]{3,2,1,0:T(1,128)} %bitcast.5, bf16[1,64,4096]{2,1,0:T(8,128)(2,1)} %defl_ref.1, bf16[1,16,5,256,256]{4,3,2,1,0:T(8,128)(2,1)} %stiff_ref.1), custom_call_target="tpu_custom_call" | custom-call | tf_op jit(solution)/shard_map/pallas_call | solution.py:340
  21.9 0.6 %copy.7 = f32[1,64,256]{2,1,0:T(8,128)} copy(f32[1,64,256]{2,1,0:T(8,128)S(1)} %shard_map.55) | data formatting | bytes 131072

commit v6 on v4

--- a/solution.py
+++ b/solution.py
@@ -12,7 +12,6 @@
 OFFSETS = [value for value in range(-RCH, RCH + 1) if value != 0]
 SEND_ORDER = sorted(OFFSETS, key=lambda value: (value < 0, abs(value)))
 NEAR_FIRST = [1, 2, -2, -1]
-ARRIVALS = [OFFSETS.index(-value) for value in SEND_ORDER]
 NT = (((1,), (1,)), ((), ()))
 NN = (((1,), (0,)), ((), ()))
 
@@ -28,7 +27,7 @@
 def kernel(
     subs, layers, off_hbm, need_hbm, place_hbm, defl_ref, stiff_ref, out_ref,
     off_ref, need_ref, place_ref, a_buf, basis, image, left_image, own_tiles, outgoing, arrived,
-    rim_out, rim_in, found_at, rim_found_at, part, part_low, shares,
+    products, rim_out, rim_in, found_at, rim_found_at, spot_at, part, part_low, shares,
     in_sem, a_sem, sub_send, sub_recv, own_send, own_recv, rim_send, rim_recv, red_send, red_recv,
 ):
     s = lax.axis_index("sub")
@@ -73,7 +72,7 @@
     edges = list(range(rim)) + list(range(tiles - rim, tiles))
 
     for k in range(count):
-        arrived[k * (overlap + 1) + overlap] = jnp.zeros((vectors, rows), arrived.dtype)
+        products[k * (overlap + 1) + overlap] = jnp.zeros((bands, vectors, rows), products.dtype)
 
     @pl.when(jnp.logical_not(has_left))
     def _():
@@ -182,19 +181,15 @@
             running = term if running is None else running + term
         image[t] = running.astype(image.dtype)
 
-    def left_of(c, blocks, lines):
+    def left_of(c):
         running = None
         for b in range(bands):
             t = c - b
-            if isinstance(t, int) and not 0 <= t < tiles:
+            if not 0 <= t < tiles:
                 continue
-            window = basis[blocks, :, pl.ds(column(t + rim), rows)]
-            term = dot_nn(window.reshape(-1, rows), a_buf[t, b])
+            term = dot_nn(basis[0, :, (t + rim) * rows : (t + rim + 1) * rows], a_buf[t, b])
             running = term if running is None else running + term
-        left_image[c, lines] = running.astype(left_image.dtype)
-
-    own = slice(0, 1), slice(0, vectors)
-    others = slice(1, slots + 1), slice(vectors, columns)
+        left_image[c, 0:vectors] = running.astype(left_image.dtype)
 
     blank = overlap
     hits = [
@@ -214,6 +209,11 @@
             for n in range(slots):
                 spot = spot + (off_ref[n, s] == offset).astype(jnp.int32) * shift[u][n]
             rim_found_at[k * len(edges) + i] = spot
+        for o in range(overlap):
+            spot = jnp.int32(0)
+            for n in range(slots):
+                spot = spot + (off_ref[n, s] == offset).astype(jnp.int32) * place_ref[0, n, 0, o]
+            spot_at[k * overlap + o] = spot
 
     group = bands - 1
     for first in range(0, tiles, group):
@@ -222,9 +222,9 @@
         for t in range(first, min(first + group, tiles)):
             if rim <= t < tiles - rim:
                 image_of(t)
-            left_of(t, *own)
+            left_of(t)
     for c in range(tiles, tiles + 2 * rim):
-        left_of(c, *own)
+        left_of(c)
     wait_pair(own_copy)
     for t in edges:
         image_of(t)
@@ -234,24 +234,42 @@
         corner = term if corner is None else corner + term
     part[0:vectors, 0:vectors] = corner
 
-    for k in ARRIVALS:
-        sub_copy(count - 1 - k, OFFSETS[count - 1 - k]).wait_recv()
+    def land(k):
+        sent = count - 1 - k
+        if isinstance(k, int):
+            offset = OFFSETS[sent]
+        else:
+            offset = sent - RCH + (sent >= RCH).astype(jnp.int32)
+        sub_copy(sent, offset).wait_recv()
         for i in range(len(edges)):
             tile = jnp.zeros((vectors, rows), arrived.dtype)
             for o in range(overlap):
-                spot = k * (overlap + 1) + o
-                tile = jnp.where(rim_found_at[k * len(edges) + i] == spot, arrived[spot], tile)
+                hit = rim_found_at[k * len(edges) + i] == k * (overlap + 1) + o
+                tile = jnp.where(hit, arrived[k * (overlap + 1) + o], tile)
             lane = i % rim * rows
             rim_out[k, i // rim, :, lane : lane + rows] = tile
-        if k != ARRIVALS[0]:
-            start_pair(rim_copy(ARRIVALS[ARRIVALS.index(k) - 1]))
-    for u in range(tiles):
+        for o in range(overlap):
+            spot = spot_at[k * overlap + o]
+            for b in range(bands):
+                term = dot_nn(arrived[k * (overlap + 1) + o], a_buf[spot, b])
+                products[k * (overlap + 1) + o, b] = term.astype(products.dtype)
+            if o == 0:
+                start_pair(rim_copy(k))
+
+    low_end, high_end = s == RCH - 1, s == subs - 1
+    land(1)
+    land(jnp.where(low_end, 2, 0))
+    land(jnp.where(jnp.logical_or(low_end, high_end), 3, 2))
+    land(jnp.where(low_end, 0, jnp.where(high_end, 2, 3)))
+    for c in range(tiles + 2 * rim):
         for n in range(slots):
-            spot = halo + u * rows
-            basis[n + 1, :, spot : spot + rows] = arrived[found_at[n * tiles + u]]
-    start_pair(rim_copy(ARRIVALS[-1]))
-    for c in range(tiles + 2 * rim):
-        left_of(c, *others)
+            total = None
+            for b in range(bands):
+                t = c - b
+                if 0 <= t < tiles:
+                    term = products[found_at[n * tiles + t], b]
+                    total = term if total is None else total + term
+            left_image[c, (n + 1) * vectors : (n + 2) * vectors] = total
     for k in range(count):
         sub_copy(k, OFFSETS[k]).wait_send()
 
@@ -333,16 +351,18 @@
         scratch_shapes=[
             *[pltpu.SMEM(table.shape, table.dtype) for table in tables],
             pltpu.VMEM((tiles, bands, rows, rows), low),
-            pltpu.VMEM((slots + 1, vectors, width + 2 * halo), low),
+            pltpu.VMEM((1, vectors, width + 2 * halo), low),
             pltpu.VMEM((tiles, vectors, rows), low),
             pltpu.VMEM((tiles + 2 * (bands // 2), columns, rows), low),
             pltpu.VMEM((tiles, vectors, rows), low),
             pltpu.VMEM((count, overlap, vectors, rows), low),
             pltpu.VMEM((count * (overlap + 1), vectors, rows), low),
+            pltpu.VMEM((count * (overlap + 1), bands, vectors, rows), low),
             pltpu.VMEM((count, 2, vectors, halo), low),
             pltpu.VMEM((count, 2, vectors, halo), low),
             pltpu.SMEM((slots * tiles,), jnp.int32),
             pltpu.SMEM((count * 2 * (bands // 2),), jnp.int32),
+            pltpu.SMEM((count * overlap,), jnp.int32),
             pltpu.VMEM((columns, columns), jnp.float32),
             pltpu.VMEM((columns, columns), low),
             pltpu.VMEM((layers - 1, share, columns), low),

time: 22.6 us -> 21.5 us (0.951)
  the two profiles are of different devices: /device:TPU:29 before, /device:TPU:0 now
where the time goes in v6:
time: 21.5 us; the launch traced here: 21.3 us
  Pallas kernels  20.7 us (96%)
  local copies, waits for them, and re-layouts  0.63 us (3%)
    pallas_call x1, Pallas kernels, on_device(): pl.pallas_call(functools.partial(kernel, subs, layers), out_shape=pltpu.V...  20.7 us
    unnamed x1, local copies, waits for them, and re-layouts  0.63 us

profile of v6, /device:TPU:0, one launch (start us, length us, event | category | flops | bytes accessed | tf_op | source)
XLA Modules:
  0.0 21.3 jit_solution(14610670456209059171)
XLA Ops:
  0.0 20.7 %shard_map.55 = f32[1,64,256]{2,1,0:T(8,128)S(1)} custom-call(s32[3,8]{1,0:T(4,128)} %bitcast.4, s32[1,3,4,8]{3,2,1,0:T(4,128)} %bitcast.3, s32[1,3,1,4]{3,2,1,0:T(1,128)} %bitcast.5, bf16[1,64,4096]{2,1,0:T(8,128)(2,1)} %defl_ref.1, bf16[1,16,5,256,256]{4,3,2,1,0:T(8,128)(2,1)} %stiff_ref.1), custom_call_target="tpu_custom_call" | custom-call | tf_op jit(solution)/shard_map/pallas_call | solution.py:346
  20.7 0.6 %copy.7 = f32[1,64,256]{2,1,0:T(8,128)} copy(f32[1,64,256]{2,1,0:T(8,128)S(1)} %shard_map.55) | data formatting | bytes 131072

commit v7 on v6

--- a/solution.py
+++ b/solution.py
@@ -99,6 +99,43 @@
                 tile = tile + match * need_ref[0, n, o, target]
             outgoing[k, o] = own_tiles[tile]
 
+    def column(t):
+        return t * rows if isinstance(t, int) else pl.multiple_of(t * rows, rows)
+
+    def image_of(t):
+        running = None
+        for b in range(bands):
+            term = dot_nt(basis[0, :, pl.ds(column(t + b), rows)], a_buf[t, b])
+            running = term if running is None else running + term
+        image[t] = running.astype(image.dtype)
+
+    def left_of(c):
+        running = None
+        for b in range(bands):
+            t = c - b
+            if not 0 <= t < tiles:
+                continue
+            term = dot_nn(basis[0, :, (t + rim) * rows : (t + rim + 1) * rows], a_buf[t, b])
+            running = term if running is None else running + term
+        left_image[c, 0:vectors] = running.astype(left_image.dtype)
+
+    group = bands - 1
+    ahead = tiles // 2 // group * group
+    waits_long = s < RCH - 1
+
+    def own_tiles_from(start, stop):
+        for first in range(start, stop, group):
+            for t in range(first, min(first + group, stop)):
+                stiff_copy(t).wait()
+            for t in range(first, min(first + group, stop)):
+                if rim <= t < tiles - rim:
+                    image_of(t)
+                left_of(t)
+
+    @pl.when(waits_long)
+    def _():
+        own_tiles_from(0, ahead)
+
     pl.semaphore_wait(barrier, count + layers - 1)
 
     def sub_copy(k, offset):
@@ -167,29 +204,9 @@
 
     start_pair(own_copy)
 
-    def column(t):
-        return t * rows if isinstance(t, int) else pl.multiple_of(t * rows, rows)
-
     def first_of(n):
         offset = off_ref[n, s]
         return (offset + RCH - (offset > 0).astype(jnp.int32)) * (overlap + 1)
-
-    def image_of(t):
-        running = None
-        for b in range(bands):
-            term = dot_nt(basis[0, :, pl.ds(column(t + b), rows)], a_buf[t, b])
-            running = term if running is None else running + term
-        image[t] = running.astype(image.dtype)
-
-    def left_of(c):
-        running = None
-        for b in range(bands):
-            t = c - b
-            if not 0 <= t < tiles:
-                continue
-            term = dot_nn(basis[0, :, (t + rim) * rows : (t + rim + 1) * rows], a_buf[t, b])
-            running = term if running is None else running + term
-        left_image[c, 0:vectors] = running.astype(left_image.dtype)
 
     blank = overlap
     hits = [
@@ -215,14 +232,11 @@
                 spot = spot + (off_ref[n, s] == offset).astype(jnp.int32) * place_ref[0, n, 0, o]
             spot_at[k * overlap + o] = spot
 
-    group = bands - 1
-    for first in range(0, tiles, group):
-        for t in range(first, min(first + group, tiles)):
-            stiff_copy(t).wait()
-        for t in range(first, min(first + group, tiles)):
-            if rim <= t < tiles - rim:
-                image_of(t)
-            left_of(t)
+    @pl.when(jnp.logical_not(waits_long))
+    def _():
+        own_tiles_from(0, ahead)
+
+    own_tiles_from(ahead, tiles)
     for c in range(tiles, tiles + 2 * rim):
         left_of(c)
     wait_pair(own_copy)
@@ -258,9 +272,9 @@
 
     low_end, high_end = s == RCH - 1, s == subs - 1
     land(1)
-    land(jnp.where(low_end, 2, 0))
-    land(jnp.where(jnp.logical_or(low_end, high_end), 3, 2))
-    land(jnp.where(low_end, 0, jnp.where(high_end, 2, 3)))
+    land(jnp.where(low_end, 3, 0))
+    land(jnp.where(low_end, 0, jnp.where(high_end, 3, 2)))
+    land(jnp.where(jnp.logical_or(low_end, high_end), 2, 3))
     for c in range(tiles + 2 * rim):
         for n in range(slots):
             total = None

time: 21.5 us -> 22 us (1.023)
  the two profiles are of different devices: /device:TPU:0 before, /device:TPU:29 now
where the time goes in v7:
time: 22 us; the launch traced here: 21.8 us
  Pallas kernels  21.1 us (96%)
  local copies, waits for them, and re-layouts  0.63 us (3%)
    pallas_call x1, Pallas kernels, on_device(): pl.pallas_call(functools.partial(kernel, subs, layers), out_shape=pltpu.V...  21.1 us
    unnamed x1, local copies, waits for them, and re-layouts  0.63 us

profile of v7, /device:TPU:29, one launch (start us, length us, event | category | flops | bytes accessed | tf_op | source)
XLA Modules:
  0.0 21.8 jit_solution(10088685860135837943)
XLA Ops:
  0.0 21.1 %shard_map.55 = f32[1,64,256]{2,1,0:T(8,128)S(1)} custom-call(s32[3,8]{1,0:T(4,128)} %bitcast.4, s32[1,3,4,8]{3,2,1,0:T(4,128)} %bitcast.3, s32[1,3,1,4]{3,2,1,0:T(1,128)} %bitcast.5, bf16[1,64,4096]{2,1,0:T(8,128)(2,1)} %defl_ref.1, bf16[1,16,5,256,256]{4,3,2,1,0:T(8,128)(2,1)} %stiff_ref.1), custom_call_target="tpu_custom_call" | custom-call | tf_op jit(solution)/shard_map/pallas_call | solution.py:360
  21.2 0.6 %copy.7 = f32[1,64,256]{2,1,0:T(8,128)} copy(f32[1,64,256]{2,1,0:T(8,128)S(1)} %shard_map.55) | data formatting | bytes 131072

commit v8 on v7

--- a/solution.py
+++ b/solution.py
@@ -120,7 +120,7 @@
         left_image[c, 0:vectors] = running.astype(left_image.dtype)
 
     group = bands - 1
-    ahead = tiles // 2 // group * group
+    ahead = group
     waits_long = s < RCH - 1
 
     def own_tiles_from(start, stop):
@@ -270,11 +270,11 @@
             if o == 0:
                 start_pair(rim_copy(k))
 
-    low_end, high_end = s == RCH - 1, s == subs - 1
-    land(1)
-    land(jnp.where(low_end, 3, 0))
-    land(jnp.where(low_end, 0, jnp.where(high_end, 3, 2)))
-    land(jnp.where(jnp.logical_or(low_end, high_end), 2, 3))
+    beside_end = jnp.logical_or(s == RCH - 1, s == subs - 1)
+    land(jnp.where(waits_long, 3, 1))
+    land(jnp.where(waits_long, 2, 0))
+    land(jnp.where(waits_long, 1, jnp.where(beside_end, 3, 2)))
+    land(jnp.where(waits_long, 0, jnp.where(beside_end, 2, 3)))
     for c in range(tiles + 2 * rim):
         for n in range(slots):
             total = None

time: 22 us -> 21.5 us (0.977)
  the two profiles are of different devices: /device:TPU:29 before, /device:TPU:0 now
where the time goes in v8:
time: 21.5 us; the launch traced here: 21.4 us
  Pallas kernels  20.7 us (96%)
  local copies, waits for them, and re-layouts  0.63 us (3%)
    pallas_call x1, Pallas kernels, on_device(): pl.pallas_call(functools.partial(kernel, subs, layers), out_shape=pltpu.V...  20.7 us
    unnamed x1, local copies, waits for them, and re-layouts  0.63 us

profile of v8, /device:TPU:0, one launch (start us, length us, event | category | flops | bytes accessed | tf_op | source)
XLA Modules:
  0.0 21.4 jit_solution(5812612291280205611)
XLA Ops:
  0.0 20.7 %shard_map.55 = f32[1,64,256]{2,1,0:T(8,128)S(1)} custom-call(s32[3,8]{1,0:T(4,128)} %bitcast.4, s32[1,3,4,8]{3,2,1,0:T(4,128)} %bitcast.3, s32[1,3,1,4]{3,2,1,0:T(1,128)} %bitcast.5, bf16[1,64,4096]{2,1,0:T(8,128)(2,1)} %defl_ref.1, bf16[1,16,5,256,256]{4,3,2,1,0:T(8,128)(2,1)} %stiff_ref.1), custom_call_target="tpu_custom_call" | custom-call | tf_op jit(solution)/shard_map/pallas_call | solution.py:360
  20.7 0.6 %copy.7 = f32[1,64,256]{2,1,0:T(8,128)} copy(f32[1,64,256]{2,1,0:T(8,128)S(1)} %shard_map.55) | data formatting | bytes 131072

commit v9 on v8

--- a/solution.py
+++ b/solution.py
@@ -262,19 +262,45 @@
                 tile = jnp.where(hit, arrived[k * (overlap + 1) + o], tile)
             lane = i % rim * rows
             rim_out[k, i // rim, :, lane : lane + rows] = tile
-        for o in range(overlap):
+
+    def multiply(k, some):
+        for o in some:
             spot = spot_at[k * overlap + o]
             for b in range(bands):
                 term = dot_nn(arrived[k * (overlap + 1) + o], a_buf[spot, b])
                 products[k * (overlap + 1) + o, b] = term.astype(products.dtype)
-            if o == 0:
-                start_pair(rim_copy(k))
+
+    def finish(k):
+        multiply(k, range(1))
+        start_pair(rim_copy(k))
+        multiply(k, range(1, overlap))
 
     beside_end = jnp.logical_or(s == RCH - 1, s == subs - 1)
-    land(jnp.where(waits_long, 3, 1))
-    land(jnp.where(waits_long, 2, 0))
-    land(jnp.where(waits_long, 1, jnp.where(beside_end, 3, 2)))
-    land(jnp.where(waits_long, 0, jnp.where(beside_end, 2, 3)))
+    together = s < RCH
+    for k in (jnp.where(waits_long, 3, 1), jnp.where(waits_long, 2, 0)):
+        land(k)
+        finish(k)
+    third = jnp.where(waits_long, 1, jnp.where(beside_end, 3, 2))
+    last = jnp.where(waits_long, 0, jnp.where(beside_end, 2, 3))
+    land(third)
+
+    @pl.when(jnp.logical_not(together))
+    def _():
+        finish(third)
+
+    land(last)
+
+    @pl.when(together)
+    def _():
+        multiply(third, range(1))
+        start_pair(rim_copy(third))
+
+    finish(last)
+
+    @pl.when(together)
+    def _():
+        multiply(third, range(1, overlap))
+
     for c in range(tiles + 2 * rim):
         for n in range(slots):
             total = None

time: 21.5 us -> 21.5 us (level)
  no operation moved by 1% of the time
where the time goes in v9:
time: 21.5 us; the launch traced here: 21.3 us
  Pallas kernels  20.6 us (96%)
  local copies, waits for them, and re-layouts  0.63 us (3%)
    pallas_call x1, Pallas kernels, on_device(): pl.pallas_call(functools.partial(kernel, subs, layers), out_shape=pltpu.V...  20.6 us
    unnamed x1, local copies, waits for them, and re-layouts  0.63 us

profile of v9, /device:TPU:0, one launch (start us, length us, event | category | flops | bytes accessed | tf_op | source)
XLA Modules:
  0.0 21.3 jit_solution(383093816394765905)
XLA Ops:
  0.0 20.6 %shard_map.55 = f32[1,64,256]{2,1,0:T(8,128)S(1)} custom-call(s32[3,8]{1,0:T(4,128)} %bitcast.4, s32[1,3,4,8]{3,2,1,0:T(4,128)} %bitcast.3, s32[1,3,1,4]{3,2,1,0:T(1,128)} %bitcast.5, bf16[1,64,4096]{2,1,0:T(8,128)(2,1)} %defl_ref.1, bf16[1,16,5,256,256]{4,3,2,1,0:T(8,128)(2,1)} %stiff_ref.1), custom_call_target="tpu_custom_call" | custom-call | tf_op jit(solution)/shard_map/pallas_call | solution.py:386
  20.6 0.6 %copy.7 = f32[1,64,256]{2,1,0:T(8,128)} copy(f32[1,64,256]{2,1,0:T(8,128)S(1)} %shard_map.55) | data formatting | bytes 131072

commit v10 on v9

--- a/solution.py
+++ b/solution.py
@@ -326,7 +326,7 @@
         part[lines, 0:vectors] = low
         part[:, lines] = below
 
-    def edge_partial(i):
+    def edge_basis(i):
         lane = i % rim * rows
         right = jnp.concatenate(
             [
@@ -334,22 +334,28 @@
                 for n in range(slots)
             ]
         )
-        return dot_nt(left_image[i if i < rim else tiles + i], right)
+        return right
 
     for k in range(count):
         wait_pair(rim_copy(k))
-    sides = None
-    for i in range(2 * rim):
-        term = edge_partial(i)
-        sides = term if sides is None else sides + term
-    part[:, vectors:] += sides
-    part_low[...] = part[...].astype(part_low.dtype)
-
+    rights = [edge_basis(i) for i in range(2 * rim)]
+    cores = 2 if layers % 2 == 0 else 1
+    chips = layers // cores
     red_copies = []
-    for step in range(1, layers):
-        peer = lax.rem(g + step, layers)
-        red_copies.append(
-            pltpu.make_async_remote_copy(
+    for away in list(range(1, chips)) + [0]:
+        chip = lax.rem(g // cores + away, chips)
+        lines = pl.ds(pl.multiple_of(chip * cores * share, cores * share), cores * share)
+        sides = None
+        for i in range(2 * rim):
+            term = dot_nt(left_image[i if i < rim else tiles + i, lines], rights[i])
+            sides = term if sides is None else sides + term
+        part[lines, vectors:] += sides
+        part_low[lines] = part[lines].astype(part_low.dtype)
+        for turn in range(cores if away else cores - 1):
+            core = turn if away else lax.rem(g + 1 + turn, cores)
+            peer = chip * cores + core
+            step = lax.rem(peer - g + layers, layers)
+            copy = pltpu.make_async_remote_copy(
                 src_ref=part_low.at[pl.ds(pl.multiple_of(peer * share, share), share)],
                 dst_ref=shares.at[step - 1],
                 send_sem=red_send.at[step - 1],
@@ -357,9 +363,8 @@
                 device_id=(s, peer),
                 device_id_type=MESH,
             )
-        )
-    for copy in red_copies:
-        copy.start()
+            copy.start()
+            red_copies.append(copy)
     for copy in red_copies:
         copy.wait()
     result = part[pl.ds(pl.multiple_of(g * share, share), share), :]

time: 21.5 us -> 21.5 us (level)
  no operation moved by 1% of the time
where the time goes in v10:
time: 21.5 us; the launch traced here: 21.3 us
  Pallas kernels  20.6 us (96%)
  local copies, waits for them, and re-layouts  0.63 us (3%)
    pallas_call x1, Pallas kernels, on_device(): pl.pallas_call(functools.partial(kernel, subs, layers), out_shape=pltpu.V...  20.6 us
    unnamed x1, local copies, waits for them, and re-layouts  0.63 us

profile of v10, /device:TPU:0, one launch (start us, length us, event | category | flops | bytes accessed | tf_op | source)
XLA Modules:
  0.0 21.3 jit_solution(4585585265788109933)
XLA Ops:
  0.0 20.6 %shard_map.55 = f32[1,64,256]{2,1,0:T(8,128)S(1)} custom-call(s32[3,8]{1,0:T(4,128)} %bitcast.4, s32[1,3,4,8]{3,2,1,0:T(4,128)} %bitcast.3, s32[1,3,1,4]{3,2,1,0:T(1,128)} %bitcast.5, bf16[1,64,4096]{2,1,0:T(8,128)(2,1)} %defl_ref.1, bf16[1,16,5,256,256]{4,3,2,1,0:T(8,128)(2,1)} %stiff_ref.1), custom_call_target="tpu_custom_call" | custom-call | tf_op jit(solution)/shard_map/pallas_call | solution.py:391
  20.6 0.6 %copy.7 = f32[1,64,256]{2,1,0:T(8,128)} copy(f32[1,64,256]{2,1,0:T(8,128)S(1)} %shard_map.55) | data formatting | bytes 131072
